TPU v7x, 32 devices: a whole 2x2x4 slice. The times are simulated.
32 devices in a mesh: wide: 8 (over y, x, core), narrow: 4 (over z).
Axes of the slice: x: 2, y: 2, z: 4, core: 2. Of those that a mesh axis runs over, the one named last changes fastest.
Arguments:
- vectors: bfloat16 [3, 4096, 128], P(None, ('wide', 'narrow')), may hold values from -18 to 18
- hessian: bfloat16 [3, 3, 61, 4096], P(None, None, None, ('wide', 'narrow')), may hold values from -0.9 to 5.4
- neighbours: int32 [60, 4096], P(None, ('wide', 'narrow')), may hold values from 0 to 415
- halo_atoms: int32 [1024], P(('wide', 'narrow')), may hold values from 0 to 127
- labels: int32 [4096], P(('wide', 'narrow')), may hold values from 0 to 15
- masses: float32 [2, 16], replicated, may hold values from 1 to 32
- rotation: float32 [2, 128, 128], replicated, may hold values from -0.5 to 0.5
Outputs:
- gram: float32 [2, 128, 128], replicated
- rotated: bfloat16 [2, 3, 4096, 128], P(None, None, ('wide', 'narrow'))
Inputs may be any that keep to these rules, and one draw needn't show every extreme that they name: `neighbours`: A row below 128 is a local atom of the domain; a row r at or above it is boundary atom (r - 128) % 32 of block (r - 128) // 32 in the 3x3 order of the steps.
All inputs are finite; a program needn't handle non-finite values.
Results may differ from a plain program's by a relative error of at most 0.003.
Values may be sent and summed in bfloat16 or wider, within the bound.
No kernel may reach another device: no remote copies, remote signals or barrier semaphores. Data moves between devices by JAX's collectives and lax.ppermute only.
A program may use at most 64 MiB of HBM per device.

v0:
```python
import functools

import jax
import jax.numpy as jnp
from jax import lax
from jax.experimental import pallas as pl
from jax.experimental.pallas import tpu as pltpu
from jax.sharding import PartitionSpec as P

AXES = ("wide", "narrow")
F32 = jnp.float32
BF16 = jnp.bfloat16
I32 = jnp.int32
VMEM = pl.BlockSpec(memory_space=pltpu.VMEM)


def iota(shape, dim):
    return lax.broadcasted_iota(I32, shape, dim)


def split(x):
    hi = x.astype(BF16)
    return hi, (x - hi.astype(F32)).astype(BF16)


def dot(a, b):
    return jnp.dot(a, b, preferred_element_type=F32)


def column(row):
    n = row.shape[1]
    return jnp.sum(jnp.where(iota((n, n), 0) == iota((n, n), 1), row, 0), axis=1, keepdims=True)


def factor_rows(labels_row, masses):
    classes = masses.shape[1]
    hit = labels_row == iota((classes, labels_row.shape[1]), 0)
    roots = lax.rsqrt(masses)
    return [
        jnp.sum(jnp.where(hit, column(roots[v : v + 1]), 0.0), axis=0, keepdims=True)
        for v in range(2)
    ]


def prepare_kernel(
    vectors_hbm, halo_hbm, labels_hbm, masses_hbm, near_hbm, hessian_hbm, rotation_hbm,
    rim_ref, vectors_ref, labels_ref, masses_ref, near_ref, hessian_ref, rotation_ref,
    halo_ref, sems,
):
    pairs = [(halo_hbm, halo_ref), (labels_hbm, labels_ref), (masses_hbm, masses_ref)]
    pairs += [(vectors_hbm.at[j], vectors_ref.at[j]) for j in range(3)]
    pairs += [(near_hbm, near_ref), (hessian_hbm, hessian_ref), (rotation_hbm, rotation_ref)]
    copies = [pltpu.make_async_copy(a, b, sems.at[i]) for i, (a, b) in enumerate(pairs)]
    for copy in copies:
        copy.start()
    for copy in copies[:6]:
        copy.wait()
    atoms, width = vectors_ref.shape[1:]
    bound = halo_ref.shape[1]
    factors = factor_rows(labels_ref[...], masses_ref[...])
    picks = column(halo_ref[...]) == iota((bound, atoms), 1)
    onehot = picks.astype(F32).astype(BF16)
    for j in range(3):
        rim_ref[j * bound : (j + 1) * bound] = dot(onehot, vectors_ref[j]).astype(BF16)
    lane = iota((bound, width), 1)
    packed = jnp.zeros((bound, width), F32)
    for v in range(2):
        rest = jnp.sum(jnp.where(picks, factors[v], 0.0), axis=1, keepdims=True)
        for k in range(3):
            part = rest.astype(BF16).astype(F32)
            packed = jnp.where(lane == 3 * v + k, part, packed)
            rest = rest - part
    fold = width // (bound // 8)
    folded = packed[:8]
    for g in range(1, bound // 8):
        folded = folded + pltpu.roll(packed[8 * g : 8 * (g + 1)], g * fold, 1)
    rim_ref[3 * bound :] = folded.astype(BF16)
    for copy in copies[6:]:
        copy.wait()


def scale_rows(blocks, exts, base):
    rows, width = blocks[0].shape
    bound = (rows - 8) // 3
    count = bound * len(blocks)
    shape = (width, 2 * width)
    spread = (iota(shape, 0) // 3 == iota(shape, 1) // width).astype(F32).astype(BF16)
    fold = width // (bound // 8)
    parts = []
    for b in blocks:
        packed = b[3 * bound :].astype(F32)
        parts += [pltpu.roll(packed, (width - g * fold) % width, 1) for g in range(bound // 8)]
    factor = dot(jnp.concatenate(parts, axis=0).astype(BF16), spread)
    for j in range(3):
        part = [b[j * bound : (j + 1) * bound] for b in blocks]
        part = jnp.concatenate(part, axis=0).astype(F32)
        part = jnp.concatenate([part, part], axis=1) * factor
        exts[j][base : base + count] = part.astype(BF16)


def one_group(near, ht_ref, onehot_scr, store, g, group):
    kpad, atoms = near.shape
    lanes = iota((kpad, onehot_scr.shape[1]), 1)
    shape = (group, group * kpad)
    own = (iota(shape, 0) == iota(shape, 1) // kpad).astype(F32).astype(BF16)
    per = group * kpad // atoms
    for a in range(group):
        at = g * group + a
        hit = near[:, at : at + 1] == lanes
        onehot_scr[a * kpad : (a + 1) * kpad, :] = hit.astype(F32).astype(BF16)
    blocks = []
    for cj in range(9):
        h = ht_ref[cj, g * group : (g + 1) * group, :]
        blocks.append(jnp.concatenate([h] * per, axis=1) * own)
    res = dot(jnp.concatenate(blocks, axis=0), onehot_scr[...])
    for cj in range(9):
        hi, lo = split(res[cj * group : (cj + 1) * group])
        store(cj // 3, cj % 3, hi, lo)


def build_kernel(
    near_in, hessian_ref, m_ref, near_ref, ht_ref, onehot_scr,
    *, n_wide, n_narrow, bound, w_base, w_step,
):
    atoms = near_in.shape[1]
    slots = hessian_ref.shape[2]
    kpad = near_ref.shape[0]
    group = 16
    p = lax.axis_index("wide")
    q = lax.axis_index("narrow")
    near = near_in[...]
    rel = near - atoms
    block = jnp.zeros_like(rel)
    for b in range(1, 9):
        block = block + (rel >= b * bound).astype(I32)
    bi = (block >= 3).astype(I32) + (block >= 6).astype(I32)
    bj = block - 3 * bi
    wp, zp = p + bi - 1, q + bj - 1
    inside = (wp >= 0) & (wp < n_wide) & (zp >= 0) & (zp < n_narrow)
    even_w, even_z = lax.rem(p, 2) == 0, lax.rem(q, 2) == 0
    up_w, down_w = jnp.where(even_w, 1, 2), jnp.where(even_w, 2, 1)
    up_z, down_z = jnp.where(even_z, 1, 2), jnp.where(even_z, 2, 1)
    sw = jnp.where(bi == 1, 0, jnp.where(bi == 2, up_w, down_w))
    sz = jnp.where(bj == 1, 0, jnp.where(bj == 2, up_z, down_z))
    head = jnp.where(sw == 0, atoms, w_base + (sw - 1) * w_step)
    placed = head + sz * bound + (rel - block * bound)
    near = jnp.where(rel < 0, near, jnp.where(inside, placed, -1))
    near_ref[kpad - 8 :, :] = jnp.full((8, atoms), -1, I32)
    near_ref[0:1, :] = iota((1, atoms), 1)
    near_ref[1:slots, :] = near
    for c in range(3):
        for j in range(3):
            h = hessian_ref[c, j].astype(F32)
            h = jnp.concatenate([h, jnp.zeros((kpad - slots, atoms), F32)], axis=0)
            h = jnp.concatenate([h] * (atoms // kpad), axis=0)
            ht_ref[c * 3 + j] = h.T.astype(BF16)
    near = near_ref[...]
    for g in range(atoms // group):

        def store(c, j, hi, lo, g=g):
            for t, part in enumerate((hi, lo)):
                at = (t * 3 + c) * atoms + g * group
                m_ref[j, at : at + group, :] = part

        one_group(near, ht_ref, onehot_scr, store, g, group)


def apply_rows(m_ref, exts, at):
    total = 0.0
    for j in range(3):
        total = total + dot(m_ref[j, :, at], exts[j])
    half = total.shape[0] // 2
    return total[:half] + total[half:]


def local_kernel(
    m_ref, vectors_ref, labels_ref, masses_ref, rim_ref, ez_ref, oz_ref,
    product_ref, factor_ref, gram_ref, reach_e_ref, reach_o_ref,
    ext_scr, vt_scr,
):
    atoms, width = vectors_ref.shape[1:]
    bound = (rim_ref.shape[0] - 8) // 3
    w_base = ext_scr.shape[1]
    factors = factor_rows(labels_ref[...], masses_ref[...])
    for v in range(2):
        f = jnp.broadcast_to(column(factors[v]), (atoms, width))
        factor_ref[v] = f
        for j in range(3):
            rows = vectors_ref[j].astype(F32) * f
            ext_scr[j, :atoms, v * width : (v + 1) * width] = rows.astype(BF16)
    scale_rows([rim_ref, ez_ref, oz_ref], [ext_scr.at[j] for j in range(3)], atoms)
    used = atoms + 3 * bound
    for j in range(3):
        ext_scr[j, used:] = jnp.zeros((w_base - used, 2 * width), BF16)
        vt_scr[:, j * atoms : (j + 1) * atoms] = vectors_ref[j].astype(F32).T
    product = apply_rows(m_ref, [ext_scr[j] for j in range(3)], slice(0, w_base))
    product_ref[...] = product
    vt = vt_scr[...]
    scaled = []
    for v in range(2):
        f = jnp.concatenate([factor_ref[v]] * 3, axis=0)
        hi, lo = split(product[:, v * width : (v + 1) * width] * f)
        both = dot(vt.astype(BF16), jnp.concatenate([hi, lo], axis=1))
        gram_ref[v] = both[:, :width] + both[:, width:]
        scaled.append(vt * jnp.concatenate([factors[v]] * 3, axis=1))
    fhi, flo = split(jnp.concatenate(scaled, axis=0))
    left = jnp.concatenate([fhi, flo], axis=0)
    for j in range(3):
        high = dot(left, m_ref[j, : 3 * atoms, w_base:])
        total = high[: 2 * width] + (high[2 * width :] + dot(fhi, m_ref[j, 3 * atoms :, w_base:]))
        cols = total.shape[1] // 2
        hi, lo = split(total)
        for v in range(2):
            rows = slice(v * width, (v + 1) * width)
            for s, ref in enumerate((reach_e_ref, reach_o_ref)):
                cut = slice(s * cols, (s + 1) * cols)
                ref[v, :width, j * cols : (j + 1) * cols] = hi[rows, cut]
                ref[v, width:, j * cols : (j + 1) * cols] = lo[rows, cut]


def partial_kernel(reach_ref, gram_ref, block_ref, *outs, last):
    ext_ref = outs[-1]
    width = block_ref.shape[2]
    bound = (block_ref.shape[1] - 8) // 3
    rows = ext_ref.shape[0] // 3
    used = 3 * bound
    blocks = [block_ref.at[z] for z in range(3)]
    scale_rows(blocks, [ext_ref.at[j * rows : (j + 1) * rows] for j in range(3)], 0)
    if used < rows:
        for j in range(3):
            ext_ref[j * rows + used : (j + 1) * rows] = jnp.zeros((rows - used, 2 * width), BF16)
    grams = []
    for v in range(2):
        both = dot(reach_ref[v], ext_ref[:, v * width : (v + 1) * width])
        grams.append(gram_ref[v] + (both[:width] + both[width:]))
    if last:
        even = lax.rem(lax.axis_index("wide"), 2) == 0
        outs[0][...] = jnp.where(even, grams[0], grams[1])
        outs[1][...] = jnp.where(even, grams[1], grams[0])
    else:
        for v in range(2):
            outs[0][v] = grams[v]


def turn_kernel(m_ref, product_ref, factor_ref, ext_e_ref, ext_o_ref, rotation_ref, out_ref):
    width = factor_ref.shape[2]
    rows = ext_e_ref.shape[0] // 3
    w_base = m_ref.shape[2] - 2 * rows
    exts = []
    for j in range(3):
        part = [ref[j * rows : (j + 1) * rows] for ref in (ext_e_ref, ext_o_ref)]
        exts.append(jnp.concatenate(part, axis=0))
    product = product_ref[...] + apply_rows(m_ref, exts, slice(w_base, None))
    for v in range(2):
        f = jnp.concatenate([factor_ref[v]] * 3, axis=0)
        hi, lo = split(product[:, v * width : (v + 1) * width] * f)
        rhi, rlo = split(rotation_ref[v])
        both = dot(hi, jnp.concatenate([rhi, rlo], axis=1))
        out_ref[v] = both[:, :width] + (both[:, width:] + dot(lo, rhi))


def finish_kernel(
    total_ref, turned_ref, vectors_ref, rotation_ref, *refs, count, own
):
    gram_hbm, out_hbm, gram_scr, out_scr, sems = refs[-5:]
    atoms = vectors_ref.shape[1]
    v = lax.rem(lax.axis_index("wide"), 2)
    v = v if own else 1 - v
    gram = total_ref[...] / count
    gram_scr[...] = gram
    copies = [pltpu.make_async_copy(gram_scr, gram_hbm.at[v], sems.at[0])]
    copies[0].start()
    hi, lo = split(gram)
    rhi, rlo = split(rotation_ref[v])
    step = dot(hi, rhi) + (dot(lo, rhi) + dot(hi, rlo))
    shi, slo = split(step)
    for j in range(3):
        vec = vectors_ref[j]
        turned = turned_ref[v, j * atoms : (j + 1) * atoms]
        out_scr[j] = (turned - (dot(vec, shi) + dot(vec, slo))).astype(BF16)
        copies.append(pltpu.make_async_copy(out_scr.at[j], out_hbm.at[v, j], sems.at[1 + j]))
        copies[-1].start()
    for copy in copies:
        copy.wait()


def swap(array, n_wide, n_narrow, place):
    pairs = []
    for p in range(n_wide):
        for q in range(n_narrow):
            a, b = place(p, q)
            pairs.append((p * n_narrow + q, a * n_narrow + b))
    return lax.ppermute(array, AXES, pairs)


def sum_stages(n_wide, n_narrow):
    bits = [(1 << k, 0) for k in range(1, n_wide.bit_length() - 1)]
    bits += [(0, 1 << k) for k in range(n_narrow.bit_length() - 1)]
    stages = []
    for k in range(0, len(bits), 2):
        steps = bits[k : k + 2]
        if steps[0][0]:
            steps = steps[::-1]
        if len(steps) == 2:
            steps.insert(0, (steps[0][0] ^ steps[1][0], steps[0][1] ^ steps[1][1]))
        stages.append(steps)
    return stages


def odd_partner(i, n):
    k = i + 1 if i % 2 else i - 1
    return k if 0 <= k < n else None


def call(kernel, out, *args, scratch=(), cost=None, space=VMEM):
    shapes = [jax.ShapeDtypeStruct(s, d) for s, d in out]
    flops, moved = cost or (1000, 1000)
    return pl.pallas_call(
        kernel,
        out_shape=shapes,
        in_specs=[space] * len(args),
        out_specs=[VMEM] * len(shapes),
        scratch_shapes=list(scratch),
        compiler_params=pltpu.CompilerParams(vmem_limit_bytes=24 * 2**20),
        cost_estimate=pl.CostEstimate(flops=flops, bytes_accessed=moved, transcendentals=0),
    )(*args)


def local(vectors, hessian, neighbours, halo_atoms, labels, masses, rotation):
    n_wide = lax.axis_size("wide")
    n_narrow = lax.axis_size("narrow")
    atoms, width = vectors.shape[1:]
    bound = halo_atoms.shape[0]
    slots = hessian.shape[2]
    kpad = -(-slots // 64) * 64
    w_base = -(-(atoms + 3 * bound) // 128) * 128
    w_step = -(-3 * bound // 128) * 128
    w_rows = 2 * w_step

    def exchange(array, place):
        return swap(array, n_wide, n_narrow, place)

    def odd_z(p, q):
        k = odd_partner(q, n_narrow)
        return (p ^ 1, q) if k is None else (p, k)

    def odd_w(p, q):
        k = odd_partner(p, n_wide)
        return (p, q ^ 1) if k is None else (k, q)

    raw = (
        vectors, halo_atoms.reshape(1, bound), labels.reshape(1, atoms), masses, neighbours,
        hessian, rotation,
    )
    hbm = pl.BlockSpec(memory_space=pltpu.HBM)
    rim, vectors, labels, masses, near, hessian, rotation = call(
        prepare_kernel,
        [((3 * bound + 8, width), BF16)] + [(a.shape, a.dtype) for i, a in enumerate(raw) if i != 1],
        *[pltpu.with_memory_space_constraint(a, pltpu.HBM) for a in raw],
        scratch=[pltpu.VMEM((1, bound), I32), pltpu.SemaphoreType.DMA((9,))],
        space=hbm,
    )
    ez = exchange(rim, lambda p, q: (p, q ^ 1))
    oz = exchange(rim, odd_z)

    def build(*refs):
        build_kernel(
            *refs, n_wide=n_wide, n_narrow=n_narrow, bound=bound, w_base=w_base, w_step=w_step
        )

    cost = (9 * atoms * 16 * kpad * (w_base + w_rows), 4 * 2**20)
    (m,) = call(
        build,
        [((3, 6 * atoms, w_base + w_rows), BF16)],
        near, hessian,
        scratch=[
            pltpu.VMEM((kpad, atoms), I32),
            pltpu.VMEM((9, atoms, atoms), BF16),
            pltpu.VMEM((16 * kpad, w_base + w_rows), BF16),
        ],
        cost=cost,
    )
    ez, oz, m = lax.optimization_barrier((ez, oz, m))
    three = jnp.stack([rim, ez, oz])
    ew = exchange(three, lambda p, q: (p ^ 1, q))
    ow = exchange(three, odd_w)
    product, factor, gram, reach_e, reach_o = call(
        local_kernel,
        [
            ((3 * atoms, 2 * width), F32),
            ((2, atoms, width), F32),
            ((2, width, width), F32),
            ((2, 2 * width, 3 * w_step), BF16),
            ((2, 2 * width, 3 * w_step), BF16),
        ],
        m, vectors, labels, masses, rim, ez, oz,
        scratch=[
            pltpu.VMEM((3, w_base, 2 * width), BF16),
            pltpu.VMEM((width, 3 * atoms), F32),
        ],
        cost=cost,
    )
    cost = (12 * width * width * w_rows, 2**20)
    rows = ((3 * w_step, 2 * width), BF16)
    square = ((width, width), F32)
    gram, ext_e = call(
        functools.partial(partial_kernel, last=False),
        [((2, width, width), F32), rows], reach_e, gram, ew, cost=cost,
    )
    mine, other, ext_o = call(
        functools.partial(partial_kernel, last=True),
        [square, square, rows], reach_o, gram, ow, cost=cost,
    )
    (turned,) = call(
        turn_kernel, [((2, 3 * atoms, width), F32)], m, product, factor, ext_e, ext_o, rotation,
        cost=(2 * 18 * atoms * w_rows * 2 * width, 4 * 2**20),
    )
    total = mine + exchange(other, lambda p, q: (p ^ 1, q))
    for k, steps in enumerate(sum_stages(n_wide, n_narrow)):
        parts = [exchange(total, lambda p, q, s=s: (p ^ s[0], q ^ s[1])) for s in steps]
        for part in parts:
            total = total + part
        if k == 0:
            total, turned = lax.optimization_barrier((total, turned))
    other = exchange(total, lambda p, q: (p ^ 1, q))
    count = 3.0 * atoms * n_wide * n_narrow
    outs = [
        jax.ShapeDtypeStruct((2, width, width), F32),
        jax.ShapeDtypeStruct((2, 3, atoms, width), BF16),
    ]

    def finish(total, held=()):
        return pl.pallas_call(
            functools.partial(finish_kernel, count=count, own=not held),
            out_shape=outs,
            in_specs=[VMEM] * 4 + [hbm] * len(held),
            out_specs=[hbm] * 2,
            scratch_shapes=[
                pltpu.VMEM((width, width), F32),
                pltpu.VMEM((3, atoms, width), BF16),
                pltpu.SemaphoreType.DMA((4,)),
            ],
            input_output_aliases={4: 0, 5: 1} if held else {},
            compiler_params=pltpu.CompilerParams(vmem_limit_bytes=24 * 2**20),
            cost_estimate=pl.CostEstimate(flops=10**6, bytes_accessed=10**6, transcendentals=0),
        )(total, turned, vectors, rotation, *held)

    return tuple(finish(other, finish(total)))


def solution(mesh):
    n_wide, n_narrow = (mesh.shape[axis] for axis in AXES)
    for size in (n_wide, n_narrow):
        assert size & (size - 1) == 0 and size > 1
    return jax.shard_map(
        local,
        mesh=mesh,
        in_specs=(
            P(None, AXES, None),
            P(None, None, None, AXES),
            P(None, AXES),
            P(AXES),
            P(AXES),
            P(),
            P(),
        ),
        out_specs=(P(), P(None, None, AXES, None)),
        check_vma=False,
    )
```

profile of v0, /device:TPU:0, one launch (start us, length us, event | category | flops | bytes accessed | tf_op | source)
XLA Modules:
  0.0 34.3 jit_solution(16670601426105480503)
XLA Ops:
  0.6 1.2 %shard_map.86 = (bf16[104,128]{1,0:T(8,128)(2,1)S(1)}, bf16[3,128,128]{2,1,0:T(8,128)(2,1)S(1)}, s32[1,128]{1,0:T(1,128)S(1)}, f32[2,16]{1,0:T(2,128)S(1)}, s32[...) custom-call(bf16[3,128,128]{2,1,0:T(8,128)(2,1)} %vectors_hbm.1, ...), custom_call_target="tpu_custom_call" | custom-call | flops 1000 | bytes 1000 | tf_op jit(solution)/shard_map/pallas_call | solution.py:318
  1.8 0.6 %collective-permute-start.1 = (bf16[104,128]{1,0:T(8,128)(2,1)S(1)}, bf16[104,128]{1,0:T(8,128)(2,1)S(1)}, u32[]{:S(2)}, u32[]{:S(2)}) collective-permute-start(bf16[104,128]{1,0:T(8,128)(2,1)S(1)} %get-tuple-element.26.rim_ref), channel_id=1, source_target_pairs={{0,4},{1,2},{2,1},{3,7},{4,0},{5,6},{6,5},{7,3},{8,12},{9,10},{10,... | collective-permute-start | bytes 79880 | tf_op jit(solution)/shard_map/ppermute | solution.py:293
  2.4 4.1 %collective-permute-start = (bf16[104,128]{1,0:T(8,128)(2,1)S(1)}, bf16[104,128]{1,0:T(8,128)(2,1)S(1)}, u32[]{:S(2)}, u32[]{:S(2)}) collective-permute-start(bf16[104,128]{1,0:T(8,128)(2,1)S(1)} %get-tuple-element.26.rim_ref), channel_id=1, source_target_pairs={{0,1},{1,0},{2,3},{3,2},{4,5},{5,4},{6,7},{7,6},{8,9},{9,8},{10,11... | collective-permute-start | bytes 79880 | tf_op jit(solution)/shard_map/ppermute | solution.py:293
  6.5 2.0 %shard_map.87.m_ref = bf16[3,768,512]{2,1,0:T(8,128)(2,1)S(1)} custom-call(s32[60,128]{1,0:T(8,128)S(1)} %get-tuple-element.27.refs_0_, bf16[3,3,61,128]{3,2,1,0:T(8,128)(2,1)S(1)} %get-tuple-element.28.refs_1_), custom_call_target="tpu_custom_call" | custom-call | flops 603979776 | bytes 4194304 | tf_op jit(solution)/shard_map/pallas_call | solution.py:318
  8.5 0.0 collective-permute-done.1.oz_ref
  8.5 0.0 collective-permute-done.ez_ref
  8.6 0.1 collective-permute-start.2
  8.6 1.9 %collective-permute-start.3 = (bf16[3,104,128]{2,1,0:T(8,128)(2,1)S(1)}, bf16[3,104,128]{2,1,0:T(8,128)(2,1)S(1)}, u32[]{:S(2)}, u32[]{:S(2)}) collective-permute-start(bf16[3,104,128]{2,1,0:T(8,128)(2,1)S(1)} %pad_maximum_fusion), channel_id=1, source_target_pairs={{0,1},{1,0},{2,3},{3,2},{4,8},{5,9},{6,10},{7,11},{8,4},{9,5},{10,... | collective-permute-start | bytes 239624 | tf_op jit(solution)/shard_map/ppermute | solution.py:293
  10.5 2.1 %shard_map.88 = (f32[384,256]{1,0:T(8,128)S(1)}, f32[2,128,128]{2,1,0:T(8,128)S(1)}, f32[2,128,128]{2,1,0:T(8,128)S(1)}, bf16[2,256,384]{2,1,0:T(8,128)(2,1)S(1)}, bf16[2,256,384]{2,1,0:T(8,128)(2,1)S(1)}) custom-call(bf16[3,768,512]{2,1,0:T(8,128)(2,1)S(1)} %shard_map.87.m_ref, bf16[3,128,128]{2,1,0:T(8,128)(2,1)S(1)} %get-tuple-element.30.vectors_ref, ...), custom_call_target="tpu_custom_call" | custom-call | flops 603979776 | bytes 4194304 | tf_op jit(solution)/shard_map/pallas_call | solution.py:318
  12.6 0.0 collective-permute-done.2.block_ref
  12.6 0.5 %shard_map.89 = (f32[2,128,128]{2,1,0:T(8,128)S(1)}, bf16[384,256]{1,0:T(8,128)(2,1)S(1)}) custom-call(bf16[2,256,384]{2,1,0:T(8,128)(2,1)S(1)} %get-tuple-element.36.reach_ref, f32[2,128,128]{2,1,0:T(8,128)S(1)} %get-tuple-element.37.gram_ref, bf16[3,104,128]{2,1,0:T(8,128)(2,1)S(1)} %collective-permute-done.2.block_ref), custom_call_target="tpu_custom_call" | custom-call | flops 50331648 | bytes 1048576 | tf_op jit(solution)/shard_map/pallas_call | solution.py:318
  13.1 0.1 collective-permute-done.3.block_ref
  13.1 0.5 %shard_map.90 = (f32[128,128]{1,0:T(8,128)S(1)}, f32[128,128]{1,0:T(8,128)S(1)}, bf16[384,256]{1,0:T(8,128)(2,1)S(1)}) custom-call(bf16[2,256,384]{2,1,0:T(8,128)(2,1)S(1)} %get-tuple-element.35.reach_ref, f32[2,128,128]{2,1,0:T(8,128)S(1)} %get-tuple-element.38.gram_ref, bf16[3,104,128]{2,1,0:T(8,128)(2,1)S(1)} %collective-permute-done.3.block_ref), custom_call_target="tpu_custom_call" | custom-call | flops 50331648 | bytes 1048576 | tf_op jit(solution)/shard_map/pallas_call | solution.py:318
  13.6 0.4 %collective-permute-start.4 = (f32[128,128]{1,0:T(8,128)S(1)}, f32[128,128]{1,0:T(8,128)S(1)}, u32[]{:S(2)}, u32[]{:S(2)}) collective-permute-start(f32[128,128]{1,0:T(8,128)S(1)} %get-tuple-element.40), channel_id=1, source_target_pairs={{0,4},{1,5},{2,6},{3,7},{4,0},{5,1},{6,2},{7,3},{8,12},{9,13},{10,... | collective-permute-start | bytes 196616 | tf_op jit(solution)/shard_map/ppermute | solution.py:293
  14.0 0.9 %collective-permute-done.4 = f32[128,128]{1,0:T(8,128)S(1)} collective-permute-done((f32[128,128]{1,0:T(8,128)S(1)}, f32[128,128]{1,0:T(8,128)S(1)}, u32[]{:S(2)}, u32[]{:S(2)}) %collective-permute-start.4) | collective-permute-done | bytes 65568 | tf_op jit(solution)/shard_map/ppermute | solution.py:293
  14.9 2.2 %collective-permute-start.7 = (f32[128,128]{1,0:T(8,128)S(1)}, f32[128,128]{1,0:T(8,128)S(1)}, u32[]{:S(2)}, u32[]{:S(2)}) collective-permute-start(f32[128,128]{1,0:T(8,128)S(1)} %add.21), channel_id=1, source_target_pairs={{0,8},{1,9},{2,10},{3,11},{4,12},{5,13},{6,14},{7,15},{8,0},{9,1},... | collective-permute-start | bytes 196616 | tf_op jit(solution)/shard_map/ppermute | solution.py:293
  17.2 0.6 %collective-permute-start.6 = (f32[128,128]{1,0:T(8,128)S(1)}, f32[128,128]{1,0:T(8,128)S(1)}, u32[]{:S(2)}, u32[]{:S(2)}) collective-permute-start(f32[128,128]{1,0:T(8,128)S(1)} %add.21), channel_id=1, source_target_pairs={{0,16},{1,17},{2,18},{3,19},{4,20},{5,21},{6,22},{7,23},{8,24},{9,... | collective-permute-start | bytes 196616 | tf_op jit(solution)/shard_map/ppermute | solution.py:293
  17.8 1.1 %collective-permute-start.5 = (f32[128,128]{1,0:T(8,128)S(1)}, f32[128,128]{1,0:T(8,128)S(1)}, u32[]{:S(2)}, u32[]{:S(2)}) collective-permute-start(f32[128,128]{1,0:T(8,128)S(1)} %add.21), channel_id=1, source_target_pairs={{0,24},{1,25},{2,26},{3,27},{4,28},{5,29},{6,30},{7,31},{8,16},{9,... | collective-permute-start | bytes 196616 | tf_op jit(solution)/shard_map/ppermute | solution.py:293
  18.8 1.0 %shard_map.91.turned_ref = f32[2,384,128]{2,1,0:T(8,128)S(1)} custom-call(bf16[3,768,512]{2,1,0:T(8,128)(2,1)S(1)} %shard_map.87.m_ref, f32[384,256]{1,0:T(8,128)S(1)} %get-tuple-element.41.product_ref, f32[2,128,128]{2,1,0:T(8,128)S(1)} %get-tuple-element.42.factor_ref, bf16[384,256]{1,0:T(8,128)(2,1)S(1)} %get-tuple-element.43.ext_e_ref, ...), custom_call_target="tpu_custom_call" | custom-call | flops 301989888 | bytes 4194304 | tf_op jit(solution)/shard_map/pallas_call | solution.py:318
  19.8 0.0 collective-permute-done.7
  19.8 2.4 %collective-permute-done.6 = f32[128,128]{1,0:T(8,128)S(1)} collective-permute-done((f32[128,128]{1,0:T(8,128)S(1)}, f32[128,128]{1,0:T(8,128)S(1)}, u32[]{:S(2)}, u32[]{:S(2)}) %collective-permute-start.6) | collective-permute-done | bytes 65568 | tf_op jit(solution)/shard_map/ppermute | solution.py:293
  22.2 0.8 %collective-permute-done.5 = f32[128,128]{1,0:T(8,128)S(1)} collective-permute-done((f32[128,128]{1,0:T(8,128)S(1)}, f32[128,128]{1,0:T(8,128)S(1)}, u32[]{:S(2)}, u32[]{:S(2)}) %collective-permute-start.5) | collective-permute-done | bytes 65568 | tf_op jit(solution)/shard_map/ppermute | solution.py:293
  22.9 1.7 %collective-permute-start.10 = (f32[128,128]{1,0:T(8,128)S(1)}, f32[128,128]{1,0:T(8,128)S(1)}, u32[]{:S(2)}, u32[]{:S(2)}) collective-permute-start(f32[128,128]{1,0:T(8,128)S(1)} %add_add_fusion.1), channel_id=1, source_target_pairs={{0,2},{1,3},{2,0},{3,1},{4,6},{5,7},{6,4},{7,5},{8,10},{9,11},{10,... | collective-permute-start | bytes 196616 | tf_op jit(solution)/shard_map/ppermute | solution.py:293
  24.7 1.2 %collective-permute-start.9 = (f32[128,128]{1,0:T(8,128)S(1)}, f32[128,128]{1,0:T(8,128)S(1)}, u32[]{:S(2)}, u32[]{:S(2)}) collective-permute-start(f32[128,128]{1,0:T(8,128)S(1)} %add_add_fusion.1), channel_id=1, source_target_pairs={{0,1},{1,0},{2,3},{3,2},{4,5},{5,4},{6,7},{7,6},{8,9},{9,8},{10,11... | collective-permute-start | bytes 196616 | tf_op jit(solution)/shard_map/ppermute | solution.py:293
  25.9 1.5 %collective-permute-start.8 = (f32[128,128]{1,0:T(8,128)S(1)}, f32[128,128]{1,0:T(8,128)S(1)}, u32[]{:S(2)}, u32[]{:S(2)}) collective-permute-start(f32[128,128]{1,0:T(8,128)S(1)} %add_add_fusion.1), channel_id=1, source_target_pairs={{0,3},{1,2},{2,1},{3,0},{4,7},{5,6},{6,5},{7,4},{8,11},{9,10},{10,... | collective-permute-start | bytes 196616 | tf_op jit(solution)/shard_map/ppermute | solution.py:293
  27.4 2.6 %collective-permute-done.10 = f32[128,128]{1,0:T(8,128)S(1)} collective-permute-done((f32[128,128]{1,0:T(8,128)S(1)}, f32[128,128]{1,0:T(8,128)S(1)}, u32[]{:S(2)}, u32[]{:S(2)}) %collective-permute-start.10) | collective-permute-done | bytes 65568 | tf_op jit(solution)/shard_map/ppermute | solution.py:293
  30.0 0.0 collective-permute-done.9
  30.0 1.9 %collective-permute-done.8 = f32[128,128]{1,0:T(8,128)S(1)} collective-permute-done((f32[128,128]{1,0:T(8,128)S(1)}, f32[128,128]{1,0:T(8,128)S(1)}, u32[]{:S(2)}, u32[]{:S(2)}) %collective-permute-start.8) | collective-permute-done | bytes 65568 | tf_op jit(solution)/shard_map/ppermute | solution.py:293
  32.0 0.1 collective-permute-start.11
  32.0 1.1 %shard_map.92 = (f32[2,128,128]{2,1,0:T(8,128)}, bf16[2,3,128,128]{3,2,1,0:T(8,128)(2,1)}) custom-call(f32[128,128]{1,0:T(8,128)S(1)} %add_add_fusion.total_ref, f32[2,384,128]{2,1,0:T(8,128)S(1)} %shard_map.91.turned_ref, bf16[3,128,128]{2,1,0:T(8,128)(2,1)S(1)} %get-tuple-element.30.vectors_ref, f32[2,128,128]{2,1,0:T(8,128)S(1)} %get-tuple-element.45.rotation_ref), custom_call_target="tpu_custom_call" | custom-call | flops 1000000 | bytes 1000000 | tf_op jit(solution)/shard_map/pallas_call | solution.py:433
  33.1 0.2 collective-permute-done.11.total_ref
  33.3 1.1 %shard_map.93 = (f32[2,128,128]{2,1,0:T(8,128)}, bf16[2,3,128,128]{3,2,1,0:T(8,128)(2,1)}) custom-call(f32[128,128]{1,0:T(8,128)S(1)} %collective-permute-done.11.total_ref, f32[2,384,128]{2,1,0:T(8,128)S(1)} %shard_map.91.turned_ref, bf16[3,128,128]{2,1,0:T(8,128)(2,1)S(1)} %get-tuple-element.30.vectors_ref, ...), custom_call_target="tpu_custom_call", output_to_operand_aliasing={{0}: (4, {}), {1}: (5, {})} | custom-call | flops 1000000 | bytes 1000000 | tf_op jit(solution)/shard_map/pallas_call | solution.py:433
  (4 shorter events, 0.0 us)
Async XLA Ops:
  1.8 6.7 %collective-permute-start.1 = (bf16[104,128]{1,0:T(8,128)(2,1)S(1)}, bf16[104,128]{1,0:T(8,128)(2,1)S(1)}, u32[]{:S(2)}, u32[]{:S(2)}) collective-permute-start(bf16[104,128]{1,0:T(8,128)(2,1)S(1)} %get-tuple-element.26.rim_ref), channel_id=1, source_target_pairs={{0,4},{1,2},{2,1},{3,7},{4,0},{5,6},{6,5},{7,3},{8,12},{9,10},{10,... | collective-permute-start | bytes 79880 | tf_op jit(solution)/shard_map/ppermute | solution.py:293
  2.4 6.2 %collective-permute-start = (bf16[104,128]{1,0:T(8,128)(2,1)S(1)}, bf16[104,128]{1,0:T(8,128)(2,1)S(1)}, u32[]{:S(2)}, u32[]{:S(2)}) collective-permute-start(bf16[104,128]{1,0:T(8,128)(2,1)S(1)} %get-tuple-element.26.rim_ref), channel_id=1, source_target_pairs={{0,1},{1,0},{2,3},{3,2},{4,5},{5,4},{6,7},{7,6},{8,9},{9,8},{10,11... | collective-permute-start | bytes 79880 | tf_op jit(solution)/shard_map/ppermute | solution.py:293
  8.6 4.0 %collective-permute-start.2 = (bf16[3,104,128]{2,1,0:T(8,128)(2,1)S(1)}, bf16[3,104,128]{2,1,0:T(8,128)(2,1)S(1)}, u32[]{:S(2)}, u32[]{:S(2)}) collective-permute-start(bf16[3,104,128]{2,1,0:T(8,128)(2,1)S(1)} %pad_maximum_fusion), channel_id=1, source_target_pairs={{0,4},{1,5},{2,6},{3,7},{4,0},{5,1},{6,2},{7,3},{8,12},{9,13},{10,... | collective-permute-start | bytes 239624 | tf_op jit(solution)/shard_map/ppermute | solution.py:293
  8.6 4.5 %collective-permute-start.3 = (bf16[3,104,128]{2,1,0:T(8,128)(2,1)S(1)}, bf16[3,104,128]{2,1,0:T(8,128)(2,1)S(1)}, u32[]{:S(2)}, u32[]{:S(2)}) collective-permute-start(bf16[3,104,128]{2,1,0:T(8,128)(2,1)S(1)} %pad_maximum_fusion), channel_id=1, source_target_pairs={{0,1},{1,0},{2,3},{3,2},{4,8},{5,9},{6,10},{7,11},{8,4},{9,5},{10,... | collective-permute-start | bytes 239624 | tf_op jit(solution)/shard_map/ppermute | solution.py:293
  13.6 1.3 %collective-permute-start.4 = (f32[128,128]{1,0:T(8,128)S(1)}, f32[128,128]{1,0:T(8,128)S(1)}, u32[]{:S(2)}, u32[]{:S(2)}) collective-permute-start(f32[128,128]{1,0:T(8,128)S(1)} %get-tuple-element.40), channel_id=1, source_target_pairs={{0,4},{1,5},{2,6},{3,7},{4,0},{5,1},{6,2},{7,3},{8,12},{9,13},{10,... | collective-permute-start | bytes 196616 | tf_op jit(solution)/shard_map/ppermute | solution.py:293
  14.9 4.8 %collective-permute-start.7 = (f32[128,128]{1,0:T(8,128)S(1)}, f32[128,128]{1,0:T(8,128)S(1)}, u32[]{:S(2)}, u32[]{:S(2)}) collective-permute-start(f32[128,128]{1,0:T(8,128)S(1)} %add.21), channel_id=1, source_target_pairs={{0,8},{1,9},{2,10},{3,11},{4,12},{5,13},{6,14},{7,15},{8,0},{9,1},... | collective-permute-start | bytes 196616 | tf_op jit(solution)/shard_map/ppermute | solution.py:293
  17.2 5.0 %collective-permute-start.6 = (f32[128,128]{1,0:T(8,128)S(1)}, f32[128,128]{1,0:T(8,128)S(1)}, u32[]{:S(2)}, u32[]{:S(2)}) collective-permute-start(f32[128,128]{1,0:T(8,128)S(1)} %add.21), channel_id=1, source_target_pairs={{0,16},{1,17},{2,18},{3,19},{4,20},{5,21},{6,22},{7,23},{8,24},{9,... | collective-permute-start | bytes 196616 | tf_op jit(solution)/shard_map/ppermute | solution.py:293
  17.8 5.2 %collective-permute-start.5 = (f32[128,128]{1,0:T(8,128)S(1)}, f32[128,128]{1,0:T(8,128)S(1)}, u32[]{:S(2)}, u32[]{:S(2)}) collective-permute-start(f32[128,128]{1,0:T(8,128)S(1)} %add.21), channel_id=1, source_target_pairs={{0,24},{1,25},{2,26},{3,27},{4,28},{5,29},{6,30},{7,31},{8,16},{9,... | collective-permute-start | bytes 196616 | tf_op jit(solution)/shard_map/ppermute | solution.py:293
  22.9 7.1 %collective-permute-start.10 = (f32[128,128]{1,0:T(8,128)S(1)}, f32[128,128]{1,0:T(8,128)S(1)}, u32[]{:S(2)}, u32[]{:S(2)}) collective-permute-start(f32[128,128]{1,0:T(8,128)S(1)} %add_add_fusion.1), channel_id=1, source_target_pairs={{0,2},{1,3},{2,0},{3,1},{4,6},{5,7},{6,4},{7,5},{8,10},{9,11},{10,... | collective-permute-start | bytes 196616 | tf_op jit(solution)/shard_map/ppermute | solution.py:293
  24.7 5.3 %collective-permute-start.9 = (f32[128,128]{1,0:T(8,128)S(1)}, f32[128,128]{1,0:T(8,128)S(1)}, u32[]{:S(2)}, u32[]{:S(2)}) collective-permute-start(f32[128,128]{1,0:T(8,128)S(1)} %add_add_fusion.1), channel_id=1, source_target_pairs={{0,1},{1,0},{2,3},{3,2},{4,5},{5,4},{6,7},{7,6},{8,9},{9,8},{10,11... | collective-permute-start | bytes 196616 | tf_op jit(solution)/shard_map/ppermute | solution.py:293
  25.9 6.1 %collective-permute-start.8 = (f32[128,128]{1,0:T(8,128)S(1)}, f32[128,128]{1,0:T(8,128)S(1)}, u32[]{:S(2)}, u32[]{:S(2)}) collective-permute-start(f32[128,128]{1,0:T(8,128)S(1)} %add_add_fusion.1), channel_id=1, source_target_pairs={{0,3},{1,2},{2,1},{3,0},{4,7},{5,6},{6,5},{7,4},{8,11},{9,10},{10,... | collective-permute-start | bytes 196616 | tf_op jit(solution)/shard_map/ppermute | solution.py:293
  32.0 1.3 %collective-permute-start.11 = (f32[128,128]{1,0:T(8,128)S(1)}, f32[128,128]{1,0:T(8,128)S(1)}, u32[]{:S(2)}, u32[]{:S(2)}) collective-permute-start(f32[128,128]{1,0:T(8,128)S(1)} %add_add_fusion.total_ref), channel_id=1, source_target_pairs={{0,4},{1,5},{2,6},{3,7},{4,0},{5,1},{6,2},{7,3},{8,12},{9,13},{10,... | collective-permute-start | bytes 196616 | tf_op jit(solution)/shard_map/ppermute | solution.py:293
where the time goes:
time: 34.5 us; the launch traced here: 34.3 us
  starting transfers between devices  15.5 us (45%)
  Pallas kernels  9.25 us (27%)
  waiting for transfers between devices  8.82 us (26%)
  between operations  0.75 us (2%)
    ppermute x12, starting transfers between devices, swap(): return lax.ppermute(array, AXES, pairs)  15.5 us
    ppermute x12, waiting for transfers between devices, swap(): return lax.ppermute(array, AXES, pairs)  8.82 us
    pallas_call x6, Pallas kernels, call(): pl.pallas_call(kernel, out_shape=shapes, in_specs=[space] * len(args), ou...  7.13 us
    pallas_call x2, Pallas kernels, finish(): pl.pallas_call(functools.partial(finish_kernel, count=count, own=not held...  2.13 us
  transfers between devices with their start and end apart: 12, of which 7 were waited for; matrix products, arithmetic and copies ran while one was open for 0% of the time, Pallas kernels for 19%

commit v1 on v0

--- a/solution.py
+++ b/solution.py
@@ -304,7 +304,11 @@
         if len(steps) == 2:
             steps.insert(0, (steps[0][0] ^ steps[1][0], steps[0][1] ^ steps[1][1]))
         stages.append(steps)
-    return stages
+    half = len(stages) // 2
+    odd = [st[:1] + st[:0:-1] if st[0][1] else st for st in stages[half:] + stages[:half]]
+    if any(len(a) != len(b) for a, b in zip(stages, odd)):
+        odd = stages
+    return [list(zip(a, b)) for a, b in zip(stages, odd)]
 
 
 def odd_partner(i, n):
@@ -417,7 +421,10 @@
     )
     total = mine + exchange(other, lambda p, q: (p ^ 1, q))
     for k, steps in enumerate(sum_stages(n_wide, n_narrow)):
-        parts = [exchange(total, lambda p, q, s=s: (p ^ s[0], q ^ s[1])) for s in steps]
+        parts = [
+            exchange(total, lambda p, q, s=s: (p ^ s[p % 2][0], q ^ s[p % 2][1]))
+            for s in steps
+        ]
         for part in parts:
             total = total + part
         if k == 0:

time: 34.5 us -> 34.5 us (level)
  transfers between devices with their start and end apart: 12 -> 12, of which waited for: 7 -> 8; matrix products, arithmetic and copies ran while one was open for 0% -> 0% of each run, Pallas kernels for 19% -> 19%
where the time goes in v1:
time: 34.5 us; the launch traced here: 34.3 us
  starting transfers between devices  15.5 us (45%)
  Pallas kernels  9.25 us (27%)
  waiting for transfers between devices  8.81 us (26%)
  between operations  0.76 us (2%)
    ppermute x12, starting transfers between devices, swap(): return lax.ppermute(array, AXES, pairs)  15.5 us
    ppermute x12, waiting for transfers between devices, swap(): return lax.ppermute(array, AXES, pairs)  8.81 us
    pallas_call x6, Pallas kernels, call(): pl.pallas_call(kernel, out_shape=shapes, in_specs=[space] * len(args), ou...  7.13 us
    pallas_call x2, Pallas kernels, finish(): pl.pallas_call(functools.partial(finish_kernel, count=count, own=not held...  2.13 us
  transfers between devices with their start and end apart: 12, of which 8 were waited for; matrix products, arithmetic and copies ran while one was open for 0% of the time, Pallas kernels for 19%

profile of v1, /device:TPU:0, one launch (start us, length us, event | category | flops | bytes accessed | tf_op | source)
XLA Modules:
  0.0 34.3 jit_solution(6031377035674901948)
XLA Ops:
  0.6 1.2 %shard_map.86 = (bf16[104,128]{1,0:T(8,128)(2,1)S(1)}, bf16[3,128,128]{2,1,0:T(8,128)(2,1)S(1)}, s32[1,128]{1,0:T(1,128)S(1)}, f32[2,16]{1,0:T(2,128)S(1)}, s32[...) custom-call(bf16[3,128,128]{2,1,0:T(8,128)(2,1)} %vectors_hbm.1, ...), custom_call_target="tpu_custom_call" | custom-call | flops 1000 | bytes 1000 | tf_op jit(solution)/shard_map/pallas_call | solution.py:322
  1.8 0.6 %collective-permute-start.1 = (bf16[104,128]{1,0:T(8,128)(2,1)S(1)}, bf16[104,128]{1,0:T(8,128)(2,1)S(1)}, u32[]{:S(2)}, u32[]{:S(2)}) collective-permute-start(bf16[104,128]{1,0:T(8,128)(2,1)S(1)} %get-tuple-element.26.rim_ref), channel_id=1, source_target_pairs={{0,4},{1,2},{2,1},{3,7},{4,0},{5,6},{6,5},{7,3},{8,12},{9,10},{10,... | collective-permute-start | bytes 79880 | tf_op jit(solution)/shard_map/ppermute | solution.py:293
  2.4 4.1 %collective-permute-start = (bf16[104,128]{1,0:T(8,128)(2,1)S(1)}, bf16[104,128]{1,0:T(8,128)(2,1)S(1)}, u32[]{:S(2)}, u32[]{:S(2)}) collective-permute-start(bf16[104,128]{1,0:T(8,128)(2,1)S(1)} %get-tuple-element.26.rim_ref), channel_id=1, source_target_pairs={{0,1},{1,0},{2,3},{3,2},{4,5},{5,4},{6,7},{7,6},{8,9},{9,8},{10,11... | collective-permute-start | bytes 79880 | tf_op jit(solution)/shard_map/ppermute | solution.py:293
  6.5 2.0 %shard_map.87.m_ref = bf16[3,768,512]{2,1,0:T(8,128)(2,1)S(1)} custom-call(s32[60,128]{1,0:T(8,128)S(1)} %get-tuple-element.27.refs_0_, bf16[3,3,61,128]{3,2,1,0:T(8,128)(2,1)S(1)} %get-tuple-element.28.refs_1_), custom_call_target="tpu_custom_call" | custom-call | flops 603979776 | bytes 4194304 | tf_op jit(solution)/shard_map/pallas_call | solution.py:322
  8.5 0.0 collective-permute-done.1.oz_ref
  8.5 0.0 collective-permute-done.ez_ref
  8.6 0.1 collective-permute-start.2
  8.6 1.9 %collective-permute-start.3 = (bf16[3,104,128]{2,1,0:T(8,128)(2,1)S(1)}, bf16[3,104,128]{2,1,0:T(8,128)(2,1)S(1)}, u32[]{:S(2)}, u32[]{:S(2)}) collective-permute-start(bf16[3,104,128]{2,1,0:T(8,128)(2,1)S(1)} %pad_maximum_fusion), channel_id=1, source_target_pairs={{0,1},{1,0},{2,3},{3,2},{4,8},{5,9},{6,10},{7,11},{8,4},{9,5},{10,... | collective-permute-start | bytes 239624 | tf_op jit(solution)/shard_map/ppermute | solution.py:293
  10.5 2.1 %shard_map.88 = (f32[384,256]{1,0:T(8,128)S(1)}, f32[2,128,128]{2,1,0:T(8,128)S(1)}, f32[2,128,128]{2,1,0:T(8,128)S(1)}, bf16[2,256,384]{2,1,0:T(8,128)(2,1)S(1)}, bf16[2,256,384]{2,1,0:T(8,128)(2,1)S(1)}) custom-call(bf16[3,768,512]{2,1,0:T(8,128)(2,1)S(1)} %shard_map.87.m_ref, bf16[3,128,128]{2,1,0:T(8,128)(2,1)S(1)} %get-tuple-element.30.vectors_ref, ...), custom_call_target="tpu_custom_call" | custom-call | flops 603979776 | bytes 4194304 | tf_op jit(solution)/shard_map/pallas_call | solution.py:322
  12.6 0.0 collective-permute-done.2.block_ref
  12.6 0.5 %shard_map.89 = (f32[2,128,128]{2,1,0:T(8,128)S(1)}, bf16[384,256]{1,0:T(8,128)(2,1)S(1)}) custom-call(bf16[2,256,384]{2,1,0:T(8,128)(2,1)S(1)} %get-tuple-element.36.reach_ref, f32[2,128,128]{2,1,0:T(8,128)S(1)} %get-tuple-element.37.gram_ref, bf16[3,104,128]{2,1,0:T(8,128)(2,1)S(1)} %collective-permute-done.2.block_ref), custom_call_target="tpu_custom_call" | custom-call | flops 50331648 | bytes 1048576 | tf_op jit(solution)/shard_map/pallas_call | solution.py:322
  13.1 0.1 collective-permute-done.3.block_ref
  13.1 0.5 %shard_map.90 = (f32[128,128]{1,0:T(8,128)S(1)}, f32[128,128]{1,0:T(8,128)S(1)}, bf16[384,256]{1,0:T(8,128)(2,1)S(1)}) custom-call(bf16[2,256,384]{2,1,0:T(8,128)(2,1)S(1)} %get-tuple-element.35.reach_ref, f32[2,128,128]{2,1,0:T(8,128)S(1)} %get-tuple-element.38.gram_ref, bf16[3,104,128]{2,1,0:T(8,128)(2,1)S(1)} %collective-permute-done.3.block_ref), custom_call_target="tpu_custom_call" | custom-call | flops 50331648 | bytes 1048576 | tf_op jit(solution)/shard_map/pallas_call | solution.py:322
  13.6 0.4 %collective-permute-start.4 = (f32[128,128]{1,0:T(8,128)S(1)}, f32[128,128]{1,0:T(8,128)S(1)}, u32[]{:S(2)}, u32[]{:S(2)}) collective-permute-start(f32[128,128]{1,0:T(8,128)S(1)} %get-tuple-element.40), channel_id=1, source_target_pairs={{0,4},{1,5},{2,6},{3,7},{4,0},{5,1},{6,2},{7,3},{8,12},{9,13},{10,... | collective-permute-start | bytes 196616 | tf_op jit(solution)/shard_map/ppermute | solution.py:293
  14.0 0.9 %collective-permute-done.4 = f32[128,128]{1,0:T(8,128)S(1)} collective-permute-done((f32[128,128]{1,0:T(8,128)S(1)}, f32[128,128]{1,0:T(8,128)S(1)}, u32[]{:S(2)}, u32[]{:S(2)}) %collective-permute-start.4) | collective-permute-done | bytes 65568 | tf_op jit(solution)/shard_map/ppermute | solution.py:293
  14.9 2.2 %collective-permute-start.7 = (f32[128,128]{1,0:T(8,128)S(1)}, f32[128,128]{1,0:T(8,128)S(1)}, u32[]{:S(2)}, u32[]{:S(2)}) collective-permute-start(f32[128,128]{1,0:T(8,128)S(1)} %add.21), channel_id=1, source_target_pairs={{0,8},{1,9},{2,10},{3,11},{4,5},{5,4},{6,7},{7,6},{8,0},{9,1},{10,... | collective-permute-start | bytes 196616 | tf_op jit(solution)/shard_map/ppermute | solution.py:293
  17.2 0.6 %collective-permute-start.6 = (f32[128,128]{1,0:T(8,128)S(1)}, f32[128,128]{1,0:T(8,128)S(1)}, u32[]{:S(2)}, u32[]{:S(2)}) collective-permute-start(f32[128,128]{1,0:T(8,128)S(1)} %add.21), channel_id=1, source_target_pairs={{0,16},{1,17},{2,18},{3,19},{4,6},{5,7},{6,4},{7,5},{8,24},{9,25},... | collective-permute-start | bytes 196616 | tf_op jit(solution)/shard_map/ppermute | solution.py:293
  17.8 1.1 %collective-permute-start.5 = (f32[128,128]{1,0:T(8,128)S(1)}, f32[128,128]{1,0:T(8,128)S(1)}, u32[]{:S(2)}, u32[]{:S(2)}) collective-permute-start(f32[128,128]{1,0:T(8,128)S(1)} %add.21), channel_id=1, source_target_pairs={{0,24},{1,25},{2,26},{3,27},{4,7},{5,6},{6,5},{7,4},{8,16},{9,17},... | collective-permute-start | bytes 196616 | tf_op jit(solution)/shard_map/ppermute | solution.py:293
  18.8 1.0 %shard_map.91.turned_ref = f32[2,384,128]{2,1,0:T(8,128)S(1)} custom-call(bf16[3,768,512]{2,1,0:T(8,128)(2,1)S(1)} %shard_map.87.m_ref, f32[384,256]{1,0:T(8,128)S(1)} %get-tuple-element.41.product_ref, f32[2,128,128]{2,1,0:T(8,128)S(1)} %get-tuple-element.42.factor_ref, bf16[384,256]{1,0:T(8,128)(2,1)S(1)} %get-tuple-element.43.ext_e_ref, ...), custom_call_target="tpu_custom_call" | custom-call | flops 301989888 | bytes 4194304 | tf_op jit(solution)/shard_map/pallas_call | solution.py:322
  19.8 0.0 collective-permute-done.7
  19.8 1.7 %collective-permute-done.6 = f32[128,128]{1,0:T(8,128)S(1)} collective-permute-done((f32[128,128]{1,0:T(8,128)S(1)}, f32[128,128]{1,0:T(8,128)S(1)}, u32[]{:S(2)}, u32[]{:S(2)}) %collective-permute-start.6) | collective-permute-done | bytes 65568 | tf_op jit(solution)/shard_map/ppermute | solution.py:293
  21.5 1.5 %collective-permute-done.5 = f32[128,128]{1,0:T(8,128)S(1)} collective-permute-done((f32[128,128]{1,0:T(8,128)S(1)}, f32[128,128]{1,0:T(8,128)S(1)}, u32[]{:S(2)}, u32[]{:S(2)}) %collective-permute-start.5) | collective-permute-done | bytes 65568 | tf_op jit(solution)/shard_map/ppermute | solution.py:293
  22.9 1.7 %collective-permute-start.10 = (f32[128,128]{1,0:T(8,128)S(1)}, f32[128,128]{1,0:T(8,128)S(1)}, u32[]{:S(2)}, u32[]{:S(2)}) collective-permute-start(f32[128,128]{1,0:T(8,128)S(1)} %add_add_fusion.1), channel_id=1, source_target_pairs={{0,2},{1,3},{2,0},{3,1},{4,12},{5,13},{6,14},{7,15},{8,10},{9,11},... | collective-permute-start | bytes 196616 | tf_op jit(solution)/shard_map/ppermute | solution.py:293
  24.7 1.2 %collective-permute-start.9 = (f32[128,128]{1,0:T(8,128)S(1)}, f32[128,128]{1,0:T(8,128)S(1)}, u32[]{:S(2)}, u32[]{:S(2)}) collective-permute-start(f32[128,128]{1,0:T(8,128)S(1)} %add_add_fusion.1), channel_id=1, source_target_pairs={{0,1},{1,0},{2,3},{3,2},{4,20},{5,21},{6,22},{7,23},{8,9},{9,8},{1... | collective-permute-start | bytes 196616 | tf_op jit(solution)/shard_map/ppermute | solution.py:293
  25.9 1.5 %collective-permute-start.8 = (f32[128,128]{1,0:T(8,128)S(1)}, f32[128,128]{1,0:T(8,128)S(1)}, u32[]{:S(2)}, u32[]{:S(2)}) collective-permute-start(f32[128,128]{1,0:T(8,128)S(1)} %add_add_fusion.1), channel_id=1, source_target_pairs={{0,3},{1,2},{2,1},{3,0},{4,28},{5,29},{6,30},{7,31},{8,11},{9,10},... | collective-permute-start | bytes 196616 | tf_op jit(solution)/shard_map/ppermute | solution.py:293
  27.4 0.8 %collective-permute-done.10 = f32[128,128]{1,0:T(8,128)S(1)} collective-permute-done((f32[128,128]{1,0:T(8,128)S(1)}, f32[128,128]{1,0:T(8,128)S(1)}, u32[]{:S(2)}, u32[]{:S(2)}) %collective-permute-start.10) | collective-permute-done | bytes 65568 | tf_op jit(solution)/shard_map/ppermute | solution.py:293
  28.2 0.8 %collective-permute-done.9 = f32[128,128]{1,0:T(8,128)S(1)} collective-permute-done((f32[128,128]{1,0:T(8,128)S(1)}, f32[128,128]{1,0:T(8,128)S(1)}, u32[]{:S(2)}, u32[]{:S(2)}) %collective-permute-start.9) | collective-permute-done | bytes 65568 | tf_op jit(solution)/shard_map/ppermute | solution.py:293
  28.9 3.0 %collective-permute-done.8 = f32[128,128]{1,0:T(8,128)S(1)} collective-permute-done((f32[128,128]{1,0:T(8,128)S(1)}, f32[128,128]{1,0:T(8,128)S(1)}, u32[]{:S(2)}, u32[]{:S(2)}) %collective-permute-start.8) | collective-permute-done | bytes 65568 | tf_op jit(solution)/shard_map/ppermute | solution.py:293
  32.0 0.1 collective-permute-start.11
  32.0 1.1 %shard_map.92 = (f32[2,128,128]{2,1,0:T(8,128)}, bf16[2,3,128,128]{3,2,1,0:T(8,128)(2,1)}) custom-call(f32[128,128]{1,0:T(8,128)S(1)} %add_add_fusion.total_ref, f32[2,384,128]{2,1,0:T(8,128)S(1)} %shard_map.91.turned_ref, bf16[3,128,128]{2,1,0:T(8,128)(2,1)S(1)} %get-tuple-element.30.vectors_ref, f32[2,128,128]{2,1,0:T(8,128)S(1)} %get-tuple-element.45.rotation_ref), custom_call_target="tpu_custom_call" | custom-call | flops 1000000 | bytes 1000000 | tf_op jit(solution)/shard_map/pallas_call | solution.py:440
  33.1 0.2 collective-permute-done.11.total_ref
  33.3 1.1 %shard_map.93 = (f32[2,128,128]{2,1,0:T(8,128)}, bf16[2,3,128,128]{3,2,1,0:T(8,128)(2,1)}) custom-call(f32[128,128]{1,0:T(8,128)S(1)} %collective-permute-done.11.total_ref, f32[2,384,128]{2,1,0:T(8,128)S(1)} %shard_map.91.turned_ref, bf16[3,128,128]{2,1,0:T(8,128)(2,1)S(1)} %get-tuple-element.30.vectors_ref, ...), custom_call_target="tpu_custom_call", output_to_operand_aliasing={{0}: (4, {}), {1}: (5, {})} | custom-call | flops 1000000 | bytes 1000000 | tf_op jit(solution)/shard_map/pallas_call | solution.py:440
  (4 shorter events, 0.0 us)
Async XLA Ops:
  1.8 6.7 %collective-permute-start.1 = (bf16[104,128]{1,0:T(8,128)(2,1)S(1)}, bf16[104,128]{1,0:T(8,128)(2,1)S(1)}, u32[]{:S(2)}, u32[]{:S(2)}) collective-permute-start(bf16[104,128]{1,0:T(8,128)(2,1)S(1)} %get-tuple-element.26.rim_ref), channel_id=1, source_target_pairs={{0,4},{1,2},{2,1},{3,7},{4,0},{5,6},{6,5},{7,3},{8,12},{9,10},{10,... | collective-permute-start | bytes 79880 | tf_op jit(solution)/shard_map/ppermute | solution.py:293
  2.4 6.2 %collective-permute-start = (bf16[104,128]{1,0:T(8,128)(2,1)S(1)}, bf16[104,128]{1,0:T(8,128)(2,1)S(1)}, u32[]{:S(2)}, u32[]{:S(2)}) collective-permute-start(bf16[104,128]{1,0:T(8,128)(2,1)S(1)} %get-tuple-element.26.rim_ref), channel_id=1, source_target_pairs={{0,1},{1,0},{2,3},{3,2},{4,5},{5,4},{6,7},{7,6},{8,9},{9,8},{10,11... | collective-permute-start | bytes 79880 | tf_op jit(solution)/shard_map/ppermute | solution.py:293
  8.6 4.0 %collective-permute-start.2 = (bf16[3,104,128]{2,1,0:T(8,128)(2,1)S(1)}, bf16[3,104,128]{2,1,0:T(8,128)(2,1)S(1)}, u32[]{:S(2)}, u32[]{:S(2)}) collective-permute-start(bf16[3,104,128]{2,1,0:T(8,128)(2,1)S(1)} %pad_maximum_fusion), channel_id=1, source_target_pairs={{0,4},{1,5},{2,6},{3,7},{4,0},{5,1},{6,2},{7,3},{8,12},{9,13},{10,... | collective-permute-start | bytes 239624 | tf_op jit(solution)/shard_map/ppermute | solution.py:293
  8.6 4.5 %collective-permute-start.3 = (bf16[3,104,128]{2,1,0:T(8,128)(2,1)S(1)}, bf16[3,104,128]{2,1,0:T(8,128)(2,1)S(1)}, u32[]{:S(2)}, u32[]{:S(2)}) collective-permute-start(bf16[3,104,128]{2,1,0:T(8,128)(2,1)S(1)} %pad_maximum_fusion), channel_id=1, source_target_pairs={{0,1},{1,0},{2,3},{3,2},{4,8},{5,9},{6,10},{7,11},{8,4},{9,5},{10,... | collective-permute-start | bytes 239624 | tf_op jit(solution)/shard_map/ppermute | solution.py:293
  13.6 1.3 %collective-permute-start.4 = (f32[128,128]{1,0:T(8,128)S(1)}, f32[128,128]{1,0:T(8,128)S(1)}, u32[]{:S(2)}, u32[]{:S(2)}) collective-permute-start(f32[128,128]{1,0:T(8,128)S(1)} %get-tuple-element.40), channel_id=1, source_target_pairs={{0,4},{1,5},{2,6},{3,7},{4,0},{5,1},{6,2},{7,3},{8,12},{9,13},{10,... | collective-permute-start | bytes 196616 | tf_op jit(solution)/shard_map/ppermute | solution.py:293
  14.9 4.8 %collective-permute-start.7 = (f32[128,128]{1,0:T(8,128)S(1)}, f32[128,128]{1,0:T(8,128)S(1)}, u32[]{:S(2)}, u32[]{:S(2)}) collective-permute-start(f32[128,128]{1,0:T(8,128)S(1)} %add.21), channel_id=1, source_target_pairs={{0,8},{1,9},{2,10},{3,11},{4,5},{5,4},{6,7},{7,6},{8,0},{9,1},{10,... | collective-permute-start | bytes 196616 | tf_op jit(solution)/shard_map/ppermute | solution.py:293
  17.2 4.3 %collective-permute-start.6 = (f32[128,128]{1,0:T(8,128)S(1)}, f32[128,128]{1,0:T(8,128)S(1)}, u32[]{:S(2)}, u32[]{:S(2)}) collective-permute-start(f32[128,128]{1,0:T(8,128)S(1)} %add.21), channel_id=1, source_target_pairs={{0,16},{1,17},{2,18},{3,19},{4,6},{5,7},{6,4},{7,5},{8,24},{9,25},... | collective-permute-start | bytes 196616 | tf_op jit(solution)/shard_map/ppermute | solution.py:293
  17.8 5.2 %collective-permute-start.5 = (f32[128,128]{1,0:T(8,128)S(1)}, f32[128,128]{1,0:T(8,128)S(1)}, u32[]{:S(2)}, u32[]{:S(2)}) collective-permute-start(f32[128,128]{1,0:T(8,128)S(1)} %add.21), channel_id=1, source_target_pairs={{0,24},{1,25},{2,26},{3,27},{4,7},{5,6},{6,5},{7,4},{8,16},{9,17},... | collective-permute-start | bytes 196616 | tf_op jit(solution)/shard_map/ppermute | solution.py:293
  22.9 5.2 %collective-permute-start.10 = (f32[128,128]{1,0:T(8,128)S(1)}, f32[128,128]{1,0:T(8,128)S(1)}, u32[]{:S(2)}, u32[]{:S(2)}) collective-permute-start(f32[128,128]{1,0:T(8,128)S(1)} %add_add_fusion.1), channel_id=1, source_target_pairs={{0,2},{1,3},{2,0},{3,1},{4,12},{5,13},{6,14},{7,15},{8,10},{9,11},... | collective-permute-start | bytes 196616 | tf_op jit(solution)/shard_map/ppermute | solution.py:293
  24.7 4.3 %collective-permute-start.9 = (f32[128,128]{1,0:T(8,128)S(1)}, f32[128,128]{1,0:T(8,128)S(1)}, u32[]{:S(2)}, u32[]{:S(2)}) collective-permute-start(f32[128,128]{1,0:T(8,128)S(1)} %add_add_fusion.1), channel_id=1, source_target_pairs={{0,1},{1,0},{2,3},{3,2},{4,20},{5,21},{6,22},{7,23},{8,9},{9,8},{1... | collective-permute-start | bytes 196616 | tf_op jit(solution)/shard_map/ppermute | solution.py:293
  25.9 6.1 %collective-permute-start.8 = (f32[128,128]{1,0:T(8,128)S(1)}, f32[128,128]{1,0:T(8,128)S(1)}, u32[]{:S(2)}, u32[]{:S(2)}) collective-permute-start(f32[128,128]{1,0:T(8,128)S(1)} %add_add_fusion.1), channel_id=1, source_target_pairs={{0,3},{1,2},{2,1},{3,0},{4,28},{5,29},{6,30},{7,31},{8,11},{9,10},... | collective-permute-start | bytes 196616 | tf_op jit(solution)/shard_map/ppermute | solution.py:293
  32.0 1.3 %collective-permute-start.11 = (f32[128,128]{1,0:T(8,128)S(1)}, f32[128,128]{1,0:T(8,128)S(1)}, u32[]{:S(2)}, u32[]{:S(2)}) collective-permute-start(f32[128,128]{1,0:T(8,128)S(1)} %add_add_fusion.total_ref), channel_id=1, source_target_pairs={{0,4},{1,5},{2,6},{3,7},{4,0},{5,1},{6,2},{7,3},{8,12},{9,13},{10,... | collective-permute-start | bytes 196616 | tf_op jit(solution)/shard_map/ppermute | solution.py:293
